TPU v7x, 32 devices: a whole 2x2x4 slice. The times are simulated.
32 devices in a mesh: groups: 2 (over y), coord: 8 (over z, x), ckpt: 2 (over core).
Axes of the slice: x: 2, y: 2, z: 4, core: 2. Of those that a mesh axis runs over, the one named last changes fastest.
Arguments:
- projection_input: bfloat16 [2, 2, 384, 4096], P('ckpt', 'groups', None, 'coord'), parts along dimension 1, may hold values from -6 to 6
- gate_output_gradient: bfloat16 [2, 2, 14336, 384], P('ckpt', 'groups', 'coord'), parts along dimension 1, may hold values from -0.59765625 to 0.59765625
- up_output_gradient: bfloat16 [2, 2, 14336, 384], P('ckpt', 'groups', 'coord'), parts along dimension 1, may hold values from -0.59765625 to 0.59765625
- hidden: bfloat16 [2, 2, 14336, 384], P('ckpt', 'groups', 'coord'), parts along dimension 1, may hold values from -6 to 6
- down_output_gradient: bfloat16 [2, 2, 384, 4096], P('ckpt', 'groups', None, 'coord'), parts along dimension 1, may hold values from -0.59765625 to 0.59765625
- gate_adapter_first: bfloat16 [2, 4096, 128], P('ckpt', 'coord'), may hold values from -0.09375 to 0.09375
- gate_adapter_second: bfloat16 [2, 14336, 128], P('ckpt', 'coord'), may hold values from -0.5 to 0.5
- up_adapter_first: bfloat16 [2, 4096, 128], P('ckpt', 'coord'), may hold values from -0.09375 to 0.09375
- up_adapter_second: bfloat16 [2, 14336, 128], P('ckpt', 'coord'), may hold values from -0.5 to 0.5
- down_adapter_first: bfloat16 [2, 14336, 128], P('ckpt', 'coord'), may hold values from -0.046875 to 0.046875
- down_adapter_second: bfloat16 [2, 4096, 128], P('ckpt', 'coord'), may hold values from -0.5 to 0.5
- random_sign_flags: int32 [16777216], P(('coord', 'ckpt')), may hold values 0 or 1
- sampled_coordinate_index: int32 [8192], replicated, may hold values from 0 to 16777215
Outputs:
- features: float32 [2, 8192], P('groups'), parts along dimension 0
There are 2 independent parts, one for each index of `groups`. A program takes and returns all parts, laid end to end along the dimension named above; an argument that names none is the same for every part. Nothing has to cross between parts.
All inputs are finite; a program needn't handle non-finite values. No bound on the sum of `random_sign_flags` on one device may be relied on, other than what follows from the above.
Results may differ from a plain program's by a relative error of at most 0.0031.
Values may be sent and summed in bfloat16 or wider, within the bound.
A program may use at most 64 MiB of HBM per device.

v0:
```python
import jax
import jax.numpy as jnp
from jax import lax
from jax.sharding import PartitionSpec as P

HAD = 16777216
adapter_scale = 2.0


def partner_2(value, axis, apart):
    mask = 2**apart
    pairs = [(source, source ^ mask) for source in range(lax.axis_size(axis))]
    return lax.ppermute(value, axis, pairs)


def walsh_table(degree):
    positions = lax.iota(jnp.int32, degree)
    parity = jnp.zeros((degree, degree), jnp.int32)
    for bit_level in range(degree.bit_length() - 1):
        parity = parity + (positions[:, None] >> bit_level & 1) * (
            positions[None, :] >> bit_level & 1
        )
    return (1 - 2 * (parity % 2)).astype(jnp.float32)


def local_walsh(signed):
    prompts = signed.shape[0]
    count = signed.shape[1]
    inner_len = min(256, count)
    outer_len = count // inner_len
    tiling = signed.reshape(prompts, outer_len, inner_len)
    tiling = jnp.einsum(
        "eoi,ji->eoj", tiling, walsh_table(inner_len), precision=lax.Precision.HIGHEST
    )
    tiling = jnp.einsum(
        "eoi,po->epi", tiling, walsh_table(outer_len), precision=lax.Precision.HIGHEST
    )
    return tiling.reshape(prompts, count)


def matrix_product(form, left, right):
    return jnp.einsum(form, left, right, preferred_element_type=jnp.float32)


def shards(
    projection_input,
    gate_output_gradient,
    up_output_gradient,
    hidden,
    down_output_gradient,
    gate_adapter_first,
    gate_adapter_second,
    up_adapter_first,
    up_adapter_second,
    down_adapter_first,
    down_adapter_second,
    random_sign_flags,
    sampled_coordinate_index,
):
    input_tensors = projection_input[0]
    gate_cotangent_value = gate_output_gradient[0]
    up_cotangent_value = up_output_gradient[0]
    hidden_input_rows = hidden[0]
    output_cotangent_value = down_output_gradient[0]
    coord_count = lax.axis_size("coord")
    partials = (
        matrix_product("nuj,jx->nux", input_tensors, gate_adapter_first[0]),
        matrix_product("nuj,jx->nux", input_tensors, up_adapter_first[0]),
        matrix_product("udo,da->uoa", hidden_input_rows, down_adapter_first[0]),
        matrix_product("udo,da->uoa", gate_cotangent_value, gate_adapter_second[0]),
        matrix_product("udo,da->uoa", up_cotangent_value, up_adapter_second[0]),
        matrix_product("nuj,jx->nux", output_cotangent_value, down_adapter_second[0]),
    )
    summed = lax.psum(
        (partials[0], partials[1], partials[2], partials[3], partials[4], partials[5]), "coord"
    )
    (
        gate_forward_pass,
        up_forward_pass,
        down_forward_pass,
        gate_backward_pass,
        up_backward_pass,
        down_backward_pass,
    ) = [part.astype(jnp.bfloat16) for part in summed]
    prompts = input_tensors.shape[0]
    adapter_rank_value = gate_adapter_first.shape[2]
    local_len = random_sign_flags.shape[0]
    pieces = [
        adapter_scale * matrix_product("ktv,ktj->kvj", input_tensors, gate_backward_pass),
        adapter_scale * matrix_product("ktv,ktj->kvj", input_tensors, up_backward_pass),
        adapter_scale * matrix_product("ktv,ktj->kvj", output_cotangent_value, down_forward_pass),
        adapter_scale * matrix_product("jpx,jxg->jpg", gate_cotangent_value, gate_forward_pass),
        adapter_scale * matrix_product("jpx,jxg->jpg", up_cotangent_value, up_forward_pass),
        adapter_scale * matrix_product("jpx,jxg->jpg", hidden_input_rows, down_backward_pass),
    ]
    filled = 3 * input_tensors.shape[2] + 3 * gate_cotangent_value.shape[1]
    pieces.append(
        jnp.zeros(
            (prompts, local_len // adapter_rank_value - filled, adapter_rank_value), jnp.float32
        )
    )
    gradient = jnp.concatenate(pieces, axis=1).reshape(prompts, local_len)
    signed = gradient * (1.0 - 2.0 * random_sign_flags.astype(jnp.float32))[None, :]
    spectrum = local_walsh(signed)
    my_coord = lax.axis_index("coord")
    ensemble_member = lax.axis_index("ckpt")
    piece_len = local_len // coord_count
    table = walsh_table(coord_count)
    mixed_data = jnp.einsum(
        "ecr,gc->egr",
        lax.all_to_all(
            spectrum.reshape(prompts, coord_count, piece_len),
            "coord",
            split_axis=1,
            concat_axis=1,
            tiled=True,
        ),
        table,
        precision=lax.Precision.HIGHEST,
    ).reshape(prompts, local_len)
    partner = partner_2(mixed_data, "ckpt", 0)
    mixed_data = jnp.where(ensemble_member == 0, mixed_data + partner, partner - mixed_data)
    group_pos = sampled_coordinate_index // (2 * local_len)
    half_pos = sampled_coordinate_index // local_len % 2
    offset = sampled_coordinate_index % local_len
    owner_pos = offset // piece_len
    flat_pos = group_pos * piece_len + offset % piece_len
    weight = jnp.where((owner_pos == my_coord) & (half_pos == ensemble_member), 1.0, 0.0)
    chosen = jnp.take(mixed_data, flat_pos, axis=1)
    contrib = chosen * weight[None, :].astype(jnp.float32) * float(HAD) ** (-0.5)
    return lax.psum(contrib, ("coord", "ckpt"))


def solution(mesh):
    in_specs = (
        P("ckpt", "groups", None, "coord"),
        P("ckpt", "groups", "coord", None),
        P("ckpt", "groups", "coord", None),
        P("ckpt", "groups", "coord", None),
        P("ckpt", "groups", None, "coord"),
        P("ckpt", "coord", None),
        P("ckpt", "coord", None),
        P("ckpt", "coord", None),
        P("ckpt", "coord", None),
        P("ckpt", "coord", None),
        P("ckpt", "coord", None),
        P(("coord", "ckpt")),
        P(),
    )
    out_specs = P("groups", None)
    return jax.shard_map(shards, mesh=mesh, in_specs=in_specs, out_specs=out_specs, check_vma=False)
```

profile of v0, /device:TPU:0, one launch (start us, length us, event | category | flops | bytes accessed | tf_op | source)
XLA Modules:
  0.0 560.0 jit_solution(11059886902752881437)
XLA Ops:
  0.0 0.0 copy-start.7
  0.0 0.6 shift-right-arithmetic_and_fusion.12
  0.6 0.6 shift-right-arithmetic_and_fusion.14
  1.2 0.5 shift-right-arithmetic_and_fusion.16
  1.7 0.6 shift-right-arithmetic_and_fusion.18
  2.3 0.6 shift-right-arithmetic_and_fusion
  2.9 0.6 shift-right-arithmetic_and_fusion.2
  3.5 0.6 shift-right-arithmetic_and_fusion.4
  4.2 0.6 shift-right-arithmetic_and_fusion.6
  4.8 0.6 shift-right-arithmetic_and_fusion.8
  5.4 0.6 shift-right-arithmetic_and_fusion.10
  6.0 2.0 convolution_bitcast_fusion.1
  7.9 2.0 convolution_bitcast_fusion.2
  9.9 1.9 convolution_bitcast_fusion.3
  11.9 2.3 fusion.59
  14.2 0.0 copy-done.6
  14.2 1.2 fusion.62
  15.4 0.0 copy-done.2
  15.4 1.3 fusion.65
  16.7 76.4 %all-reduce.2 = (bf16[1,384,128]{2,1,0:T(8,128)(2,1)}, bf16[1,384,128]{2,1,0:T(8,128)(2,1)}, bf16[1,384,128]{2,1,0:T(8,128)(2,1)}, bf16[1,384,128]{2,1,0:T(8,128...) all-reduce(f32[1,384,128]{2,1,0:T(8,128)} %fusion.59, ...), channel_id=1, replica_groups=mesh['groups'=2,'coord'=8,'ckpt'=2] {'coord'}, use_global_device_ids=true, to_apply=%region_0.0 | all-reduce | flops 294912 | bytes 1769472 | tf_op jit(solution)/shard_map/psum | solution.py:74
  93.1 2.0 fusion.58
  95.1 1.9 fusion.56
  96.9 1.9 fusion.54
  98.8 2.5 fusion.39
  101.3 1.5 fusion.41
  102.8 0.0 copy-done.9
  102.8 1.5 fusion.43
  104.3 0.9 broadcast_dynamic-update-slice_fusion
  105.2 5.7 %copy.15 = f32[1,8192,128]{2,1,0:T(8,128)} copy(f32[1,8192,128]{1,2,0:T(8,128)} %broadcast_dynamic-update-slice_fusion) | data formatting | bytes 8388608 | tf_op jit(solution)/shard_map/concatenate | solution.py:102
  110.9 6.0 %bitcast_multiply_fusion = f32[1048576]{0:T(1024)} fusion(f32[1,8192,128]{2,1,0:T(8,128)} %copy.15, s32[1048576]{0:T(1024)} %param.24), kind=kLoop, calls=%fused_computation.43 | loop fusion | flops 4194304 | bytes 12582912 | tf_op jit(solution)/shard_map/mul | solution.py:103
  116.9 0.0 copy-start.26
  116.9 5.2 reshape.436
  122.2 0.0 copy-start.11
  122.3 6.0 %fusion.81 = f32[4096,256]{1,0:T(8,128)S(1)} fusion(f32[4096,256]{1,0:T(8,128)} %reshape.436, s32[256]{0:T(256)S(1)} %copy-done.22, s32[256]{0:T(256)S(1)} %copy-done.23, s32[256]{0:T(256)S(1)} %copy-done.24, s32[256]{0:T(256)S(1)} %copy-done.25, s32[256]{0:T(256)S(1)} %copy-done.26, s32[256]{0:T(256)S(1)} %copy-done.27, s32[256]{0:T(256)S(1)} %copy-done.28, ...), kind=kOutput, calls=%fused_computation.94 | convolution fusion | flops 3223126016 | bytes 8396800 | tf_op jit(solution)/shard_map/eoi,ji->eoj/dot_general | solution.py:32
  128.5 149.6 %fusion.4 = f32[4096,256]{1,0:T(8,128)} fusion(f32[4096,256]{1,0:T(8,128)S(1)} %fusion.81, s32[4096]{0:T(1024)S(1)} %get-tuple-element.19, s32[4096]{0:T(1024)S(1)} %copy-done.11, s32[4096]{0:T(1024)S(1)} %copy-done.12, s32[4096]{0:T(1024)S(1)} %copy-done.13, s32[4096]{0:T(1024)S(1)} %copy-done.14, s32[4096]{0:T(1024)S(1)} %copy-done.15, ...), kind=kOutput, calls=%fused_computation.9 | convolution fusion | flops 52160364544 | bytes 8585216 | tf_op jit(solution)/shard_map/eoi,po->epi/dot_general | solution.py:35
  278.1 8.4 %transpose.90 = f32[1,8,131072]{2,0,1:T(1,128)} reshape(f32[4096,256]{1,0:T(8,128)} %fusion.4) | data formatting | bytes 8388608 | tf_op jit(solution)/shard_map/reshape;reshape;eoi,po->epi/transpose | solution.py:112
  286.5 4.6 all-to-all-start
  291.1 83.1 %all-to-all-done = f32[1,8,131072]{2,0,1:T(1,128)} async-done(((f32[1,8,131072]{2,0,1:T(1,128)}), f32[1,8,131072]{2,0,1:T(1,128)}, u32[]{:S(2)}, u32[]{:S(2)}) %all-to-all-start) | async-done | bytes 4194336 | tf_op jit(solution)/shard_map/all_to_all | solution.py:111
  374.1 8.0 %convolution_bitcast_fusion = f32[1,1,8,131072]{3,2,1,0:T(8,128)S(1)} fusion(f32[1,8,131072]{2,0,1:T(1,128)} %all-to-all-done, s32[8]{0:T(128)S(1)} %get-tuple-element.31, s32[8]{0:T(128)S(1)} %get-tuple-element.32, s32[8]{0:T(128)S(1)} %shift-right-arithmetic_and_fusion.22), kind=kOutput, calls=%fused_computation.1 | convolution fusion | flops 100664512 | bytes 8388704 | tf_op jit(solution)/shard_map/ecr,gc->egr/dot_general | solution.py:109
  382.2 0.0 copy-start.8
  382.2 6.3 %copy.18 = f32[1,1,8,131072]{3,1,2,0:T(1,128)} copy(f32[1,1,8,131072]{3,2,1,0:T(8,128)S(1)} %convolution_bitcast_fusion) | data formatting | bytes 8388608
  388.5 0.0 collective-permute-start
  388.5 0.1 fusion.130
  388.6 7.4 %collective-permute-done = f32[1,1048576]{1,0:T(1,128)} collective-permute-done((f32[1,1048576]{1,0:T(1,128)}, f32[1,1048576]{1,0:T(1,128)}, u32[]{:S(2)}, u32[]{:S(2)}) %collective-permute-start) | collective-permute-done | bytes 4194336 | tf_op jit(solution)/shard_map/ppermute | solution.py:13
  396.0 7.2 %broadcast_select_fusion = f32[1,1048576]{1,0:T(1,128)} fusion(pred[]{:T(512)S(6)} %eq.25, f32[1,1048576]{1,0:T(1,128)} %collective-permute-done, f32[1,1048576]{1,0:T(1,128)} %bitcast.135), kind=kLoop, calls=%fused_computation.40 | loop fusion | flops 3145728 | bytes 12582913 | tf_op jit(solution)/shard_map/jit(_where)/select_n | solution.py:122
  403.2 96.3 %gather_fusion = f32[8192]{0:T(1024)S(1)} fusion(f32[1048576]{0:T(1024)} %bitcast.133, s32[8192]{0:T(1024)S(1)} %fusion.130), kind=kCustom, calls=%fused_computation | custom fusion | bytes 98304 | tf_op jit(solution)/shard_map/jit(_take)/gather | solution.py:129
  499.5 0.1 multiply_multiply_fusion
  499.6 60.0 %psum.55 = f32[1,8192]{1,0:T(1,128)} all-reduce(f32[1,8192]{1,0:T(1,128)S(1)} %bitcast.136), channel_id=1, replica_groups=mesh['groups'=2,'coord'=8,'ckpt'=2] {'coord','ckpt'}, use_global_device_ids=true, to_apply=%region_6.7 | all-reduce | flops 8192 | bytes 65536 | tf_op jit(solution)/shard_map/psum | solution.py:131
  (55 shorter events, 0.1 us)
Async XLA Ops:
  0.0 11.9 %copy-start = (bf16[1,1,1792,384]{3,2,1,0:T(8,128)(2,1)S(1)}, bf16[1,1,1792,384]{3,2,1,0:T(8,128)(2,1)}, u32[]{:S(2)}) copy-start(bf16[1,1,1792,384]{3,2,1,0:T(8,128)(2,1)} %param.14) | copy-start | bytes 4128772
  0.0 14.2 %copy-start.1 = (bf16[1,1,1792,384]{3,2,1,0:T(8,128)(2,1)S(1)}, bf16[1,1,1792,384]{3,2,1,0:T(8,128)(2,1)}, u32[]{:S(2)}) copy-start(bf16[1,1,1792,384]{3,2,1,0:T(8,128)(2,1)} %param.15) | copy-start | bytes 4128772
  0.0 14.2 %copy-start.6 = (bf16[1,1792,128]{2,1,0:T(8,128)(2,1)S(1)}, bf16[1,1792,128]{2,1,0:T(8,128)(2,1)}, u32[]{:S(2)}) copy-start(bf16[1,1792,128]{2,1,0:T(8,128)(2,1)} %param.21) | copy-start | bytes 1376260
  0.0 15.4 %copy-start.2 = (bf16[1,1,1792,384]{3,2,1,0:T(8,128)(2,1)S(1)}, bf16[1,1,1792,384]{3,2,1,0:T(8,128)(2,1)}, u32[]{:S(2)}) copy-start(bf16[1,1,1792,384]{3,2,1,0:T(8,128)(2,1)} %param.16) | copy-start | bytes 4128772
  0.0 15.4 %copy-start.7 = (bf16[1,1792,128]{2,1,0:T(8,128)(2,1)S(1)}, bf16[1,1792,128]{2,1,0:T(8,128)(2,1)}, u32[]{:S(2)}) copy-start(bf16[1,1792,128]{2,1,0:T(8,128)(2,1)} %param.22) | copy-start | bytes 1376260
  11.9 81.2 %copy-start.4 = (bf16[1,1,384,512]{3,2,1,0:T(8,128)(2,1)S(1)}, bf16[1,1,384,512]{3,2,1,0:T(8,128)(2,1)}, u32[]{:S(2)}) copy-start(bf16[1,1,384,512]{3,2,1,0:T(8,128)(2,1)} %param.13) | copy-start | bytes 1179652
  14.2 82.7 %copy-start.5 = (bf16[1,1,384,512]{3,2,1,0:T(8,128)(2,1)S(1)}, bf16[1,1,384,512]{3,2,1,0:T(8,128)(2,1)}, u32[]{:S(2)}) copy-start(bf16[1,1,384,512]{3,2,1,0:T(8,128)(2,1)} %param.17) | copy-start | bytes 1179652
  93.1 8.2 %copy-start.10 = (bf16[1,384,128]{2,1,0:T(8,128)(2,1)S(1)}, bf16[1,384,128]{2,1,0:T(8,128)(2,1)}, u32[]{:S(2)}) copy-start(bf16[1,384,128]{2,1,0:T(8,128)(2,1)} %get-tuple-element.9) | copy-start | bytes 294916
  93.1 9.7 %copy-start.3 = (bf16[1,1,1792,384]{3,2,1,0:T(8,128)(2,1)S(1)}, bf16[1,1,1792,384]{3,2,1,0:T(8,128)(2,1)}, u32[]{:S(2)}) copy-start(bf16[1,1,1792,384]{3,2,1,0:T(8,128)(2,1)} %param.16) | copy-start | bytes 4128772
  93.1 9.7 %copy-start.9 = (bf16[1,384,128]{2,1,0:T(8,128)(2,1)S(1)}, bf16[1,384,128]{2,1,0:T(8,128)(2,1)}, u32[]{:S(2)}) copy-start(bf16[1,384,128]{2,1,0:T(8,128)(2,1)} %get-tuple-element.10) | copy-start | bytes 294916
  116.9 5.3 copy-start.22
  116.9 5.3 copy-start.23
  116.9 5.3 copy-start.24
  116.9 5.3 copy-start.25
  116.9 5.3 copy-start.26
  116.9 5.3 copy-start.27
  116.9 5.3 copy-start.28
  116.9 5.3 copy-start.29
  122.2 6.2 %copy-start.11 = (s32[4096]{0:T(1024)S(1)}, s32[4096]{0:T(1024)}, u32[]{:S(2)}) copy-start(s32[4096]{0:T(1024)} %get-tuple-element.20) | copy-start | bytes 49156
  122.2 6.2 %copy-start.12 = (s32[4096]{0:T(1024)S(1)}, s32[4096]{0:T(1024)}, u32[]{:S(2)}) copy-start(s32[4096]{0:T(1024)} %get-tuple-element.21) | copy-start | bytes 49156
  122.2 6.2 %copy-start.13 = (s32[4096]{0:T(1024)S(1)}, s32[4096]{0:T(1024)}, u32[]{:S(2)}) copy-start(s32[4096]{0:T(1024)} %get-tuple-element.22) | copy-start | bytes 49156
  122.2 6.2 %copy-start.14 = (s32[4096]{0:T(1024)S(1)}, s32[4096]{0:T(1024)}, u32[]{:S(2)}) copy-start(s32[4096]{0:T(1024)} %get-tuple-element.23) | copy-start | bytes 49156
  122.2 6.2 %copy-start.15 = (s32[4096]{0:T(1024)S(1)}, s32[4096]{0:T(1024)}, u32[]{:S(2)}) copy-start(s32[4096]{0:T(1024)} %get-tuple-element.24) | copy-start | bytes 49156
  122.3 6.2 %copy-start.16 = (s32[4096]{0:T(1024)S(1)}, s32[4096]{0:T(1024)}, u32[]{:S(2)}) copy-start(s32[4096]{0:T(1024)} %get-tuple-element.25) | copy-start | bytes 49156
  122.3 6.2 %copy-start.17 = (s32[4096]{0:T(1024)S(1)}, s32[4096]{0:T(1024)}, u32[]{:S(2)}) copy-start(s32[4096]{0:T(1024)} %get-tuple-element.26) | copy-start | bytes 49156
  122.3 6.2 %copy-start.18 = (s32[4096]{0:T(1024)S(1)}, s32[4096]{0:T(1024)}, u32[]{:S(2)}) copy-start(s32[4096]{0:T(1024)} %get-tuple-element.27) | copy-start | bytes 49156
  122.3 6.2 %copy-start.19 = (s32[4096]{0:T(1024)S(1)}, s32[4096]{0:T(1024)}, u32[]{:S(2)}) copy-start(s32[4096]{0:T(1024)} %get-tuple-element.28) | copy-start | bytes 49156
  122.3 6.2 %copy-start.20 = (s32[4096]{0:T(1024)S(1)}, s32[4096]{0:T(1024)}, u32[]{:S(2)}) copy-start(s32[4096]{0:T(1024)} %get-tuple-element.29) | copy-start | bytes 49156
  122.3 6.2 %copy-start.21 = (s32[4096]{0:T(1024)S(1)}, s32[4096]{0:T(1024)}, u32[]{:S(2)}) copy-start(s32[4096]{0:T(1024)} %get-tuple-element.30) | copy-start | bytes 49156
  286.5 87.6 %all-to-all-start = ((f32[1,8,131072]{2,0,1:T(1,128)}), f32[1,8,131072]{2,0,1:T(1,128)}, u32[]{:S(2)}, u32[]{:S(2)}) async-start(f32[1,8,131072]{2,0,1:T(1,128)} %transpose.90), calls=%async_computation | async-start | bytes 8388608 | tf_op jit(solution)/shard_map/all_to_all | solution.py:111
  382.2 6.3 %copy-start.8 = (s32[8192]{0:T(1024)S(1)}, s32[8192]{0:T(1024)}, u32[]{:S(2)}) copy-start(s32[8192]{0:T(1024)} %param.25) | copy-start | bytes 98308
  388.5 7.5 %collective-permute-start = (f32[1,1048576]{1,0:T(1,128)}, f32[1,1048576]{1,0:T(1,128)}, u32[]{:S(2)}, u32[]{:S(2)}) collective-permute-start(f32[1,1048576]{1,0:T(1,128)} %bitcast.134), channel_id=1, source_target_pairs={{0,1},{1,0},{2,3},{3,2},{4,5},{5,4},{6,7},{7,6},{8,9},{9,8},{10,11... | collective-permute-start | bytes 12582920 | tf_op jit(solution)/shard_map/ppermute | solution.py:13
where the time goes:
time: 571 us; the launch traced here: 560 us
  matrix products  186 us (33%)
  blocking collectives  136 us (24%)
  local copies, waits for them, and re-layouts  123 us (22%)
  waiting for transfers between devices  90.5 us (16%)
  other arithmetic  19.3 us (3%)
    dot_general x1, matrix products, local_walsh(): jnp.einsum('eoi,po->epi', tiling, walsh_table(outer_len), precision=lax.P...  150 us
    gather x1, local copies, waits for them, and re-layouts, shards(): chosen = jnp.take(mixed_data, flat_pos, axis=1)  96.3 us
    all_to_all x1, waiting for transfers between devices, shards(): lax.all_to_all(spectrum.reshape(prompts, coord_count, piece_len), 'coord'...  83.1 us
    psum x1, blocking collectives, shards(): lax.psum((partials[0], partials[1], partials[2], partials[3], partials[4]...  76.4 us
    psum x1, blocking collectives, shards(): return lax.psum(contrib, ('coord', 'ckpt'))  60 us
    dot_general x12, matrix products, matrix_product(): return jnp.einsum(form, left, right, preferred_element_type=jnp.float32)  21.9 us
  transfers between devices with their start and end apart: 2, of which 2 were waited for; matrix products, arithmetic and copies ran while one was open for 0% of the time, Pallas kernels for 0%

commit v1 on v0

--- a/solution.py
+++ b/solution.py
@@ -5,6 +5,12 @@
 
 HAD = 16777216
 adapter_scale = 2.0
+
+
+def exchange_blocks(x, axis, split, join):
+    pieces = jnp.split(x, lax.axis_size(axis), axis=split)
+    incoming = lax.all_to_all(jnp.stack(pieces), axis, 0, 0)
+    return jnp.concatenate(incoming, axis=join)
 
 
 def partner_2(value, axis, apart):
@@ -108,13 +114,7 @@
     table = walsh_table(coord_count)
     mixed_data = jnp.einsum(
         "ecr,gc->egr",
-        lax.all_to_all(
-            spectrum.reshape(prompts, coord_count, piece_len),
-            "coord",
-            split_axis=1,
-            concat_axis=1,
-            tiled=True,
-        ),
+        exchange_blocks(spectrum.reshape(prompts, coord_count, piece_len), "coord", 1, 1),
         table,
         precision=lax.Precision.HIGHEST,
     ).reshape(prompts, local_len)

time: 571 us -> 594 us (1.040)
  local copies, waits for them, and re-layouts: 123 us -> 147 us
    unnamed x61 -> x70, local copies, waits for them, and re-layouts: 6.42 us -> 30.4 us
where the time goes in v1:
time: 594 us; the launch traced here: 583 us
  matrix products  184 us (31%)
  local copies, waits for them, and re-layouts  147 us (25%)
  blocking collectives  137 us (23%)
  waiting for transfers between devices  90.2 us (15%)
  other arithmetic  19.4 us (3%)
    dot_general x1, matrix products, local_walsh(): jnp.einsum('eoi,po->epi', tiling, walsh_table(outer_len), precision=lax.P...  148 us
    gather x1, local copies, waits for them, and re-layouts, shards(): chosen = jnp.take(mixed_data, flat_pos, axis=1)  96.3 us
    all_to_all x1, waiting for transfers between devices, exchange_blocks(): incoming = lax.all_to_all(jnp.stack(pieces), axis, 0, 0)  82.8 us
    psum x1, blocking collectives, shards(): lax.psum((partials[0], partials[1], partials[2], partials[3], partials[4]...  76.6 us
    psum x1, blocking collectives, shards(): return lax.psum(contrib, ('coord', 'ckpt'))  60 us
    unnamed x70, local copies, waits for them, and re-layouts  30.4 us
    dot_general x12, matrix products, matrix_product(): return jnp.einsum(form, left, right, preferred_element_type=jnp.float32)  22 us
  transfers between devices with their start and end apart: 2, of which 2 were waited for; matrix products, arithmetic and copies ran while one was open for 0% of the time, Pallas kernels for 0%

profile of v1, /device:TPU:0, one launch (start us, length us, event | category | flops | bytes accessed | tf_op | source)
XLA Modules:
  0.0 582.5 jit_solution(746780758157271625)
XLA Ops:
  0.0 0.6 shift-right-arithmetic_and_fusion.12
  0.6 0.6 shift-right-arithmetic_and_fusion.14
  1.2 0.6 shift-right-arithmetic_and_fusion.16
  1.8 0.5 shift-right-arithmetic_and_fusion.18
  2.3 0.6 shift-right-arithmetic_and_fusion
  2.9 0.6 shift-right-arithmetic_and_fusion.2
  3.6 0.6 shift-right-arithmetic_and_fusion.4
  4.2 0.6 shift-right-arithmetic_and_fusion.6
  4.8 0.6 shift-right-arithmetic_and_fusion.8
  5.4 0.6 shift-right-arithmetic_and_fusion.10
  6.0 2.0 convolution_bitcast_fusion.1
  8.0 2.0 convolution_bitcast_fusion.2
  10.0 2.0 convolution_bitcast_fusion.3
  11.9 2.3 fusion.59
  14.3 1.2 fusion.62
  15.5 1.3 fusion.65
  16.8 76.6 %all-reduce.2 = (bf16[1,384,128]{2,1,0:T(8,128)(2,1)}, bf16[1,384,128]{2,1,0:T(8,128)(2,1)}, bf16[1,384,128]{2,1,0:T(8,128)(2,1)}, bf16[1,384,128]{2,1,0:T(8,128...) all-reduce(f32[1,384,128]{2,1,0:T(8,128)} %fusion.59, ...), channel_id=1, replica_groups=mesh['groups'=2,'coord'=8,'ckpt'=2] {'coord'}, use_global_device_ids=true, to_apply=%region_0.0 | all-reduce | flops 294912 | bytes 1769472 | tf_op jit(solution)/shard_map/psum | solution.py:80
  93.4 2.0 fusion.58
  95.3 1.9 fusion.56
  97.2 1.9 fusion.54
  99.1 2.4 fusion.39
  101.6 1.5 fusion.41
  103.1 1.6 fusion.43
  104.7 0.9 broadcast_dynamic-update-slice_fusion
  105.6 5.7 copy.14
  111.3 6.0 %bitcast_multiply_fusion = f32[1048576]{0:T(1024)} fusion(f32[1,8192,128]{2,1,0:T(8,128)} %copy.14, s32[1048576]{0:T(1024)} %param.24), kind=kLoop, calls=%fused_computation.43 | loop fusion | flops 4194304 | bytes 12582912 | tf_op jit(solution)/shard_map/mul | solution.py:109
  117.3 5.2 reshape.438
  122.7 6.1 %fusion.89 = f32[4096,256]{1,0:T(8,128)S(1)} fusion(f32[4096,256]{1,0:T(8,128)} %reshape.438, s32[256]{0:T(256)S(1)} %copy-done.23, s32[256]{0:T(256)S(1)} %copy-done.24, s32[256]{0:T(256)S(1)} %copy-done.25, s32[256]{0:T(256)S(1)} %copy-done.26, s32[256]{0:T(256)S(1)} %copy-done.27, s32[256]{0:T(256)S(1)} %copy-done.28, s32[256]{0:T(256)S(1)} %copy-done.29, ...), kind=kOutput, calls=%fused_computation.110 | convolution fusion | flops 3223126016 | bytes 8396800 | tf_op jit(solution)/shard_map/eoi,ji->eoj/dot_general | solution.py:38
  128.9 148.0 %fusion.4 = f32[4096,256]{1,0:T(8,128)} fusion(f32[4096,256]{1,0:T(8,128)S(1)} %fusion.89, s32[4096]{0:T(1024)S(1)} %get-tuple-element.19, s32[4096]{0:T(1024)S(1)} %copy-done.12, s32[4096]{0:T(1024)S(1)} %copy-done.13, s32[4096]{0:T(1024)S(1)} %copy-done.14, s32[4096]{0:T(1024)S(1)} %copy-done.15, s32[4096]{0:T(1024)S(1)} %copy-done.16, ...), kind=kOutput, calls=%fused_computation.9 | convolution fusion | flops 52160364544 | bytes 8585216 | tf_op jit(solution)/shard_map/eoi,po->epi/dot_general | solution.py:41
  276.9 4.9 transpose.82
  281.8 3.3 fusion.75
  285.1 3.5 fusion.74
  288.5 3.4 fusion.73
  292.0 3.4 fusion.72
  295.4 3.4 fusion.71
  298.9 3.4 fusion.70
  302.3 3.5 fusion.69
  305.8 3.5 fusion.68
  309.2 4.6 all-to-all-start
  313.8 82.8 %all-to-all-done = f32[8,1,1,131072]{3,2,1,0:T(1,128)} async-done(((f32[8,1,1,131072]{3,2,1,0:T(1,128)}), f32[8,1,1,131072]{3,2,1,0:T(1,128)}, u32[]{:S(2)}, u32[]{:S(2)}) %all-to-all-start) | async-done | bytes 4194336 | tf_op jit(solution)/shard_map/all_to_all | solution.py:12
  396.6 8.0 %convolution_bitcast_fusion = f32[1,1,8,131072]{3,2,1,0:T(8,128)S(1)} fusion(f32[8,1,1,131072]{3,2,1,0:T(1,128)} %all-to-all-done, s32[8]{0:T(128)S(1)} %get-tuple-element.31, s32[8]{0:T(128)S(1)} %get-tuple-element.32, s32[8]{0:T(128)S(1)} %shift-right-arithmetic_and_fusion.22), kind=kOutput, calls=%fused_computation.1 | convolution fusion | flops 100664512 | bytes 8388704 | tf_op jit(solution)/shard_map/ecr,gc->egr/dot_general | solution.py:115
  404.7 6.3 %copy.16 = f32[1,1,8,131072]{3,1,2,0:T(1,128)} copy(f32[1,1,8,131072]{3,2,1,0:T(8,128)S(1)} %convolution_bitcast_fusion) | data formatting | bytes 8388608
  411.0 0.1 fusion.138
  411.0 7.4 %collective-permute-done = f32[1,1048576]{1,0:T(1,128)} collective-permute-done((f32[1,1048576]{1,0:T(1,128)}, f32[1,1048576]{1,0:T(1,128)}, u32[]{:S(2)}, u32[]{:S(2)}) %collective-permute-start) | collective-permute-done | bytes 4194336 | tf_op jit(solution)/shard_map/ppermute | solution.py:19
  418.5 7.2 %broadcast_select_fusion = f32[1,1048576]{1,0:T(1,128)} fusion(pred[]{:T(512)S(6)} %eq.25, f32[1,1048576]{1,0:T(1,128)} %collective-permute-done, f32[1,1048576]{1,0:T(1,128)} %bitcast.167), kind=kLoop, calls=%fused_computation.40 | loop fusion | flops 3145728 | bytes 12582913 | tf_op jit(solution)/shard_map/jit(_where)/select_n | solution.py:122
  425.7 96.3 %gather_fusion = f32[8192]{0:T(1024)S(1)} fusion(f32[1048576]{0:T(1024)} %bitcast.165, s32[8192]{0:T(1024)S(1)} %fusion.138), kind=kCustom, calls=%fused_computation | custom fusion | bytes 98304 | tf_op jit(solution)/shard_map/jit(_take)/gather | solution.py:129
  522.0 0.1 multiply_multiply_fusion
  522.1 60.0 %psum.55 = f32[1,8192]{1,0:T(1,128)} all-reduce(f32[1,8192]{1,0:T(1,128)S(1)} %bitcast.168), channel_id=1, replica_groups=mesh['groups'=2,'coord'=8,'ckpt'=2] {'coord','ckpt'}, use_global_device_ids=true, to_apply=%region_6.7 | all-reduce | flops 8192 | bytes 65536 | tf_op jit(solution)/shard_map/psum | solution.py:131
  (65 shorter events, 0.1 us)
Async XLA Ops:
  0.0 11.9 %copy-start = (bf16[1,1,1792,384]{3,2,1,0:T(8,128)(2,1)S(1)}, bf16[1,1,1792,384]{3,2,1,0:T(8,128)(2,1)}, u32[]{:S(2)}) copy-start(bf16[1,1,1792,384]{3,2,1,0:T(8,128)(2,1)} %param.14) | copy-start | bytes 4128772
  0.0 14.2 %copy-start.2 = (bf16[1,1,1792,384]{3,2,1,0:T(8,128)(2,1)S(1)}, bf16[1,1,1792,384]{3,2,1,0:T(8,128)(2,1)}, u32[]{:S(2)}) copy-start(bf16[1,1,1792,384]{3,2,1,0:T(8,128)(2,1)} %param.15) | copy-start | bytes 4128772
  0.0 14.2 %copy-start.7 = (bf16[1,1792,128]{2,1,0:T(8,128)(2,1)S(1)}, bf16[1,1792,128]{2,1,0:T(8,128)(2,1)}, u32[]{:S(2)}) copy-start(bf16[1,1792,128]{2,1,0:T(8,128)(2,1)} %param.21) | copy-start | bytes 1376260
  0.0 15.5 %copy-start.3 = (bf16[1,1,1792,384]{3,2,1,0:T(8,128)(2,1)S(1)}, bf16[1,1,1792,384]{3,2,1,0:T(8,128)(2,1)}, u32[]{:S(2)}) copy-start(bf16[1,1,1792,384]{3,2,1,0:T(8,128)(2,1)} %param.16) | copy-start | bytes 4128772
  0.0 15.5 %copy-start.8 = (bf16[1,1792,128]{2,1,0:T(8,128)(2,1)S(1)}, bf16[1,1792,128]{2,1,0:T(8,128)(2,1)}, u32[]{:S(2)}) copy-start(bf16[1,1792,128]{2,1,0:T(8,128)(2,1)} %param.22) | copy-start | bytes 1376260
  11.9 81.4 %copy-start.5 = (bf16[1,1,384,512]{3,2,1,0:T(8,128)(2,1)S(1)}, bf16[1,1,384,512]{3,2,1,0:T(8,128)(2,1)}, u32[]{:S(2)}) copy-start(bf16[1,1,384,512]{3,2,1,0:T(8,128)(2,1)} %param.13) | copy-start | bytes 1179652
  14.3 83.0 %copy-start.6 = (bf16[1,1,384,512]{3,2,1,0:T(8,128)(2,1)S(1)}, bf16[1,1,384,512]{3,2,1,0:T(8,128)(2,1)}, u32[]{:S(2)}) copy-start(bf16[1,1,384,512]{3,2,1,0:T(8,128)(2,1)} %param.17) | copy-start | bytes 1179652
  93.4 8.2 %copy-start.11 = (bf16[1,384,128]{2,1,0:T(8,128)(2,1)S(1)}, bf16[1,384,128]{2,1,0:T(8,128)(2,1)}, u32[]{:S(2)}) copy-start(bf16[1,384,128]{2,1,0:T(8,128)(2,1)} %get-tuple-element.9) | copy-start | bytes 294916
  93.4 9.7 %copy-start.4 = (bf16[1,1,1792,384]{3,2,1,0:T(8,128)(2,1)S(1)}, bf16[1,1,1792,384]{3,2,1,0:T(8,128)(2,1)}, u32[]{:S(2)}) copy-start(bf16[1,1,1792,384]{3,2,1,0:T(8,128)(2,1)} %param.16) | copy-start | bytes 4128772
  93.4 9.7 %copy-start.10 = (bf16[1,384,128]{2,1,0:T(8,128)(2,1)S(1)}, bf16[1,384,128]{2,1,0:T(8,128)(2,1)}, u32[]{:S(2)}) copy-start(bf16[1,384,128]{2,1,0:T(8,128)(2,1)} %get-tuple-element.10) | copy-start | bytes 294916
  117.3 5.3 copy-start.23
  117.3 5.3 copy-start.24
  117.3 5.3 copy-start.25
  117.3 5.3 copy-start.26
  117.3 5.3 copy-start.27
  117.3 5.3 copy-start.28
  117.3 5.3 copy-start.29
  117.3 5.3 copy-start.30
  122.6 6.2 %copy-start.12 = (s32[4096]{0:T(1024)S(1)}, s32[4096]{0:T(1024)}, u32[]{:S(2)}) copy-start(s32[4096]{0:T(1024)} %get-tuple-element.20) | copy-start | bytes 49156
  122.6 6.2 %copy-start.13 = (s32[4096]{0:T(1024)S(1)}, s32[4096]{0:T(1024)}, u32[]{:S(2)}) copy-start(s32[4096]{0:T(1024)} %get-tuple-element.21) | copy-start | bytes 49156
  122.7 6.2 %copy-start.14 = (s32[4096]{0:T(1024)S(1)}, s32[4096]{0:T(1024)}, u32[]{:S(2)}) copy-start(s32[4096]{0:T(1024)} %get-tuple-element.22) | copy-start | bytes 49156
  122.7 6.2 %copy-start.15 = (s32[4096]{0:T(1024)S(1)}, s32[4096]{0:T(1024)}, u32[]{:S(2)}) copy-start(s32[4096]{0:T(1024)} %get-tuple-element.23) | copy-start | bytes 49156
  122.7 6.2 %copy-start.16 = (s32[4096]{0:T(1024)S(1)}, s32[4096]{0:T(1024)}, u32[]{:S(2)}) copy-start(s32[4096]{0:T(1024)} %get-tuple-element.24) | copy-start | bytes 49156
  122.7 6.2 %copy-start.17 = (s32[4096]{0:T(1024)S(1)}, s32[4096]{0:T(1024)}, u32[]{:S(2)}) copy-start(s32[4096]{0:T(1024)} %get-tuple-element.25) | copy-start | bytes 49156
  122.7 6.2 %copy-start.18 = (s32[4096]{0:T(1024)S(1)}, s32[4096]{0:T(1024)}, u32[]{:S(2)}) copy-start(s32[4096]{0:T(1024)} %get-tuple-element.26) | copy-start | bytes 49156
  122.7 6.2 %copy-start.19 = (s32[4096]{0:T(1024)S(1)}, s32[4096]{0:T(1024)}, u32[]{:S(2)}) copy-start(s32[4096]{0:T(1024)} %get-tuple-element.27) | copy-start | bytes 49156
  122.7 6.2 %copy-start.20 = (s32[4096]{0:T(1024)S(1)}, s32[4096]{0:T(1024)}, u32[]{:S(2)}) copy-start(s32[4096]{0:T(1024)} %get-tuple-element.28) | copy-start | bytes 49156
  122.7 6.2 %copy-start.21 = (s32[4096]{0:T(1024)S(1)}, s32[4096]{0:T(1024)}, u32[]{:S(2)}) copy-start(s32[4096]{0:T(1024)} %get-tuple-element.29) | copy-start | bytes 49156
  122.7 6.2 %copy-start.22 = (s32[4096]{0:T(1024)S(1)}, s32[4096]{0:T(1024)}, u32[]{:S(2)}) copy-start(s32[4096]{0:T(1024)} %get-tuple-element.30) | copy-start | bytes 49156
  309.2 87.4 %all-to-all-start = ((f32[8,1,1,131072]{3,2,1,0:T(1,128)}), f32[8,1,1,131072]{3,2,1,0:T(1,128)}, u32[]{:S(2)}, u32[]{:S(2)}) async-start(f32[8,1,1,131072]{3,2,1,0:T(1,128)} %fusion.68), calls=%async_computation | async-start | bytes 8388608 | tf_op jit(solution)/shard_map/all_to_all | solution.py:12
  404.7 6.3 %copy-start.9 = (s32[8192]{0:T(1024)S(1)}, s32[8192]{0:T(1024)}, u32[]{:S(2)}) copy-start(s32[8192]{0:T(1024)} %param.25) | copy-start | bytes 98308
  411.0 7.5 %collective-permute-start = (f32[1,1048576]{1,0:T(1,128)}, f32[1,1048576]{1,0:T(1,128)}, u32[]{:S(2)}, u32[]{:S(2)}) collective-permute-start(f32[1,1048576]{1,0:T(1,128)} %bitcast.166), channel_id=1, source_target_pairs={{0,1},{1,0},{2,3},{3,2},{4,5},{5,4},{6,7},{7,6},{8,9},{9,8},{10,11... | collective-permute-start | bytes 12582920 | tf_op jit(solution)/shard_map/ppermute | solution.py:19
  425.7 156.5 %copy-start.1 = (bf16[1,1,1792,384]{3,2,1,0:T(8,128)(2,1)S(1)}, bf16[1,1,1792,384]{3,2,1,0:T(8,128)(2,1)}, u32[]{:S(2)}) copy-start(bf16[1,1,1792,384]{3,2,1,0:T(8,128)(2,1)} %param.14) | copy-start | bytes 4128772
